TPU v7x, 32 devices: a whole 2x2x4 slice. The times are simulated.
32 devices in a mesh: chain: 16 (over z, y, core), aux: 2 (over x).
Axes of the slice: x: 2, y: 2, z: 4, core: 2. Of those that a mesh axis runs over, the one named last changes fastest.
Arguments:
- occupied: bfloat16 [2048, 1152], P('chain'), may hold values from -0.1875 to 0.1875
- virtual: bfloat16 [2048, 1152], P('chain'), may hold values from -0.1875 to 0.1875
- three_centre: bfloat16 [32, 2048, 1152], P('aux', 'chain'), may hold values from -6 to 6
- kernel: bfloat16 [32, 32], P('aux'), may hold values from -1 to 1
- profile: int32 [16], replicated, may hold values from 2 to 4
- atom_map: int32 [32], P('aux'), may hold values from 0 to 15
Outputs:
- band_gradient: float32 [2048, 1152], P(('chain', 'aux'))
- polarization: float32 [32, 32], P('aux')
All inputs are finite; a program needn't handle non-finite values.
Results may differ from a plain program's by a relative error of at most 0.0042.
Values may be sent and summed in bfloat16 or wider, within the bound.
No kernel may reach another device: no remote copies, remote signals or barrier semaphores. Data moves between devices by JAX's collectives and lax.ppermute only.
A program may use at most 128 MiB of HBM per device.

v0:
```python
import math
import jax
import jax.numpy as jnp
from jax import lax
from jax.sharding import PartitionSpec as P


def passed_along(block, axis, distance):
    devices = range(lax.axis_size(axis))
    route = [(i - distance, i) for i in devices if i - distance in devices]
    return lax.ppermute(block, axis, route)


def shift_blocks(matrix, offset, block_size):
    if offset == 0:
        return matrix
    padding = jnp.zeros(matrix.shape[:-1] + (abs(offset) * block_size,), matrix.dtype)
    if offset > 0:
        return jnp.concatenate([padding, matrix[..., : -offset * block_size]], -1)
    return jnp.concatenate([matrix[..., -offset * block_size :], padding], -1)


def body(occupied, virtual, three_centre, kernel, profile, atom_map):
    block_size = occupied.shape[0]
    band_cols = occupied.shape[1]
    slots_total = band_cols // block_size
    spread = (slots_total - 1) // 2
    nblocks = lax.axis_size("chain")
    position = lax.axis_index("chain")
    slot_ids = jnp.arange(slots_total, dtype=jnp.int32)
    block_ids = jnp.arange(nblocks, dtype=jnp.int32)
    others = position + slot_ids - spread
    neighbours = jnp.sum(jnp.where(block_ids[None, :] == others[:, None], profile[None, :], 0), 1)
    own_width = jnp.sum(jnp.where(block_ids == position, profile, 0))
    allowed = jnp.abs(slot_ids - spread) <= jnp.minimum(own_width, neighbours)
    column_keep = jnp.repeat(allowed, block_size)
    zero_half = jnp.zeros((), jnp.bfloat16)
    occ_masked = jnp.where(column_keep[None, :], occupied, zero_half)
    vir_masked = jnp.where(column_keep[None, :], virtual, zero_half)
    both_bands = jnp.stack([occ_masked, vir_masked])
    fetched = []
    for slot_index in range(slots_total):
        if slot_index == spread:
            fetched.append(both_bands)
        else:
            fetched.append(passed_along(both_bands, "chain", spread - slot_index))
    stack_occ = jnp.concatenate(
        [shift_blocks(fetched[k][0], k - spread, block_size) for k in range(slots_total)], 0
    )
    stack_vir = jnp.concatenate(
        [shift_blocks(fetched[k][1], k - spread, block_size) for k in range(slots_total)], 0
    )
    aux_here = three_centre.shape[0]
    aux_total = kernel.shape[1]
    screen = jnp.abs(atom_map - position) <= nblocks // 4
    local = jnp.where(column_keep[None, None, :] & screen[:, None, None], three_centre, zero_half)
    screened = local.reshape(aux_here * block_size, band_cols)
    coupled = jnp.dot(screened, stack_occ, preferred_element_type=jnp.float32).astype(jnp.bfloat16)
    coupled = coupled.reshape(aux_here, block_size * band_cols)
    partner = jnp.dot(screened, stack_vir, preferred_element_type=jnp.float32).astype(jnp.bfloat16)
    partner = partner.reshape(aux_here, block_size, band_cols)
    piece = lax.all_gather(partner, "aux", axis=0, tiled=True)
    piece_rows = piece.shape[0]
    columns = piece.reshape(piece_rows, block_size * band_cols)
    products = lax.dot_general(
        coupled, columns, (((1,), (1,)), ((), ())), preferred_element_type=jnp.float32
    )
    polar_part = products
    response_sum = jnp.dot(kernel, columns, preferred_element_type=jnp.float32)
    polar_part, response_sum = (polar_part, response_sum)
    polarization = lax.psum(polar_part, "chain") * (
        1.0 / math.sqrt(block_size * nblocks * band_cols)
    )
    response = response_sum.astype(jnp.bfloat16).reshape(aux_here * block_size, band_cols)
    partials = lax.dot_general(
        screened, response, (((0,), (0,)), ((), ())), preferred_element_type=jnp.float32
    )
    partials = partials.reshape(slots_total, block_size, band_cols)
    gathered_sum = partials[spread]
    for slot_index in range(slots_total):
        if slot_index != spread:
            moved = shift_blocks(partials[slot_index], spread - slot_index, block_size)
            gathered_sum = gathered_sum + passed_along(moved, "chain", slot_index - spread)
    gathered_sum = lax.psum_scatter(gathered_sum, "aux", scatter_dimension=0, tiled=True)
    scale_grad = 1.0 / math.sqrt(block_size * aux_total)
    band_gradient = (
        jnp.where(column_keep[None, :], gathered_sum, jnp.zeros((), jnp.float32)) * scale_grad
    )
    return (band_gradient, polarization)


def solution(mesh):
    placed = (
        P("chain", None),
        P("chain", None),
        P("aux", "chain", None),
        P("aux", None),
        P(),
        P("aux"),
    )
    return jax.shard_map(
        body,
        mesh=mesh,
        in_specs=placed,
        out_specs=(P(("chain", "aux"), None), P("aux", None)),
        check_vma=False,
    )
```

profile of v0, /device:TPU:0, one launch (start us, length us, event | category | flops | bytes accessed | tf_op | source)
XLA Modules:
  0.0 369.4 jit_solution(13112788531242796778)
XLA Ops:
  7.2 1.3 fusion.12
  11.3 1.3 collective-permute-start.7
  12.6 1.3 collective-permute-start.6
  13.9 1.3 collective-permute-start.5
  15.2 1.3 collective-permute-start.4
  16.5 3.1 collective-permute-start.3
  20.3 2.8 broadcast_select_fusion
  23.2 7.3 %collective-permute-done.7 = bf16[2,128,1152]{2,1,0:T(8,128)(2,1)S(1)} collective-permute-done((bf16[2,128,1152]{2,1,0:T(8,128)(2,1)S(1)}, bf16[2,128,1152]{2,1,0:T(8,128)(2,1)S(1)}, u32[]{:S(2)}, u32[]{:S(2)}) %collective-permute-start.7) | collective-permute-done | bytes 589856 | tf_op jit(solution)/shard_map/ppermute | solution.py:11
  30.4 2.8 collective-permute-start.2
  33.3 6.0 %collective-permute-start.1 = (bf16[2,128,1152]{2,1,0:T(8,128)(2,1)S(1)}, bf16[2,128,1152]{2,1,0:T(8,128)(2,1)S(1)}, u32[]{:S(2)}, u32[]{:S(2)}) collective-permute-start(bf16[2,128,1152]{2,1,0:T(8,128)(2,1)S(1)} %pad_maximum_fusion), channel_id=1, source_target_pairs={{0,6},{2,8},{4,10},{6,12},{8,14},{10,16},{12,18},{14,20},{16,22},{... | collective-permute-start | bytes 1769480 | tf_op jit(solution)/shard_map/ppermute | solution.py:11
  39.3 24.2 %collective-permute-start = (bf16[2,128,1152]{2,1,0:T(8,128)(2,1)S(1)}, bf16[2,128,1152]{2,1,0:T(8,128)(2,1)S(1)}, u32[]{:S(2)}, u32[]{:S(2)}) collective-permute-start(bf16[2,128,1152]{2,1,0:T(8,128)(2,1)S(1)} %pad_maximum_fusion), channel_id=1, source_target_pairs={{0,8},{2,10},{4,12},{6,14},{8,16},{10,18},{12,20},{14,22},{16,24},... | collective-permute-start | bytes 1769480 | tf_op jit(solution)/shard_map/ppermute | solution.py:11
  63.7 4.2 %collective-permute-done.2 = bf16[2,128,1152]{2,1,0:T(8,128)(2,1)S(1)} collective-permute-done((bf16[2,128,1152]{2,1,0:T(8,128)(2,1)S(1)}, bf16[2,128,1152]{2,1,0:T(8,128)(2,1)S(1)}, u32[]{:S(2)}, u32[]{:S(2)}) %collective-permute-start.2) | collective-permute-done | bytes 589856 | tf_op jit(solution)/shard_map/ppermute | solution.py:11
  68.2 6.0 %collective-permute-done.1 = bf16[2,128,1152]{2,1,0:T(8,128)(2,1)S(1)} collective-permute-done((bf16[2,128,1152]{2,1,0:T(8,128)(2,1)S(1)}, bf16[2,128,1152]{2,1,0:T(8,128)(2,1)S(1)}, u32[]{:S(2)}, u32[]{:S(2)}) %collective-permute-start.1) | collective-permute-done | bytes 589856 | tf_op jit(solution)/shard_map/ppermute | solution.py:11
  75.8 8.6 %convolution_convert_fusion.2 = bf16[2048,1152]{1,0:T(8,128)(2,1)} fusion(bf16[2048,1152]{1,0:T(8,128)(2,1)S(1)} %bitcast.58, bf16[1152,1152]{1,0:T(8,128)(2,1)S(1)} %pad_dynamic-update-slice_fusion.8), kind=kOutput, calls=%fused_computation.3 | convolution fusion | flops 5438177280 | bytes 12091392 | tf_op jit(solution)/shard_map/dot_general | solution.py:60
  84.7 122.4 %all-gather.2.cloned.1.call-done = bf16[32,128,1152]{2,1,0:T(8,128)(2,1)} async-done(((bf16[16,128,1152]{2,1,0:T(8,128)(2,1)}), bf16[32,128,1152]{2,1,0:T(8,128)(2,1)}) %all-gather.2.cloned.1.call-update) | async-done | bytes 9437200 | tf_op jit(solution)/shard_map/all_gather | solution.py:62
  207.0 12.8 %copy.8 = bf16[4,8,128,1152]{3,1,2,0:T(8,128)(2,1)} copy(bf16[4,8,128,1152]{3,2,1,0:T(8,128)(2,1)} %bitcast.56) | data formatting | bytes 18874368
  219.8 7.2 %fusion = bf16[16,147456]{1,0:T(8,128)(2,1)} fusion(bf16[16,32]{1,0:T(8,128)(2,1)S(1)} %copy-done, bf16[32,147456]{1,0:T(8,128)(2,1)} %bitcast.54), kind=kOutput, calls=%fused_computation.1 | convolution fusion | flops 153354240 | bytes 14156800 | tf_op jit(solution)/shard_map/dot_general | solution.py:69
  227.0 5.3 %reshape.79 = bf16[2048,1152]{1,0:T(8,128)(2,1)} reshape(bf16[16,147456]{1,0:T(8,128)(2,1)} %fusion) | data formatting | bytes 9437184 | tf_op jit(solution)/shard_map/reshape | solution.py:74
  232.2 10.3 %fusion.17 = f32[1152,1152]{1,0:T(8,128)S(1)} fusion(bf16[2048,1152]{1,0:T(8,128)(2,1)} %bitcast.59, bf16[2048,1152]{1,0:T(8,128)(2,1)} %reshape.79), kind=kOutput, calls=%fused_computation.67 | convolution fusion | flops 5435817984 | bytes 14745600 | tf_op jit(solution)/shard_map/dot_general | solution.py:75
  242.8 3.4 collective-permute-start.15
  246.2 1.3 collective-permute-start.8
  247.6 2.4 collective-permute-start.14
  251.5 4.3 %collective-permute-start.13 = (f32[128,1152]{1,0:T(8,128)S(1)}, f32[128,1152]{1,0:T(8,128)S(1)}, u32[]{:S(2)}, u32[]{:S(2)}) collective-permute-start(f32[128,1152]{1,0:T(8,128)S(1)} %concatenate.92), channel_id=1, source_target_pairs={{0,4},{2,6},{4,8},{6,10},{8,12},{10,14},{12,16},{14,18},{16,20},{1... | collective-permute-start | bytes 1769480 | tf_op jit(solution)/shard_map/ppermute | solution.py:11
  256.0 3.8 %collective-permute-done.15 = f32[128,1152]{1,0:T(8,128)S(1)} collective-permute-done((f32[128,1152]{1,0:T(8,128)S(1)}, f32[128,1152]{1,0:T(8,128)S(1)}, u32[]{:S(2)}, u32[]{:S(2)}) %collective-permute-start.15) | collective-permute-done | bytes 589856 | tf_op jit(solution)/shard_map/ppermute | solution.py:11
  261.2 3.1 collective-permute-done.8
  264.3 1.3 collective-permute-start.12
  267.1 27.6 %collective-permute-done.13 = f32[128,1152]{1,0:T(8,128)S(1)} collective-permute-done((f32[128,1152]{1,0:T(8,128)S(1)}, f32[128,1152]{1,0:T(8,128)S(1)}, u32[]{:S(2)}, u32[]{:S(2)}) %collective-permute-start.13) | collective-permute-done | bytes 589856 | tf_op jit(solution)/shard_map/ppermute | solution.py:11
  295.8 10.4 %convolution_convert_fusion.1 = bf16[2048,1152]{1,0:T(8,128)(2,1)} fusion(bf16[2048,1152]{1,0:T(8,128)(2,1)} %bitcast.60, bf16[1152,1152]{1,0:T(8,128)(2,1)S(1)} %pad_dynamic-update-slice_fusion), kind=kOutput, calls=%fused_computation.2 | convolution fusion | flops 5438177280 | bytes 12091392 | tf_op jit(solution)/shard_map/dot_general | solution.py:58
  306.2 5.3 %reshape.80 = bf16[16,147456]{1,0:T(8,128)(2,1)} reshape(bf16[2048,1152]{1,0:T(8,128)(2,1)} %convolution_convert_fusion.1) | data formatting | bytes 9437184 | tf_op jit(solution)/shard_map/reshape | solution.py:59
  311.5 7.8 %fusion.18 = f32[16,32]{1,0:T(8,128)S(1)} fusion(bf16[16,147456]{1,0:T(8,128)(2,1)} %reshape.80, bf16[32,147456]{1,0:T(8,128)(2,1)} %bitcast.55), kind=kOutput, calls=%fused_computation.68 | convolution fusion | flops 150994944 | bytes 14157824 | tf_op jit(solution)/shard_map/dot_general | solution.py:65
  319.3 40.9 %psum.7 = f32[16,32]{1,0:T(8,128)S(1)} all-reduce(f32[16,32]{1,0:T(8,128)S(1)} %fusion.18), channel_id=1, replica_groups=mesh['chain'=16,'aux'=2] {'chain'}, use_global_device_ids=true, to_apply=%region_3.4 | all-reduce | flops 512 | bytes 4096 | tf_op jit(solution)/shard_map/psum | solution.py:71
  360.9 1.7 select_multiply_fusion
  (90 shorter events, 12.0 us)
Async XLA Ops:
  7.2 212.6 %copy-start = (bf16[16,32]{1,0:T(8,128)(2,1)S(1)}, bf16[16,32]{1,0:T(8,128)(2,1)}, u32[]{:S(2)}) copy-start(bf16[16,32]{1,0:T(8,128)(2,1)} %param.9) | copy-start | bytes 3076
  7.2 199.8 %all-gather.2.cloned.1.call-start = ((), (), s32[]{:S(2)}) async-start(), calls=%async_computation.1 | async-start | bytes 14155776 | tf_op jit(solution)/shard_map/all_gather | solution.py:62
  11.3 19.1 %collective-permute-start.7 = (bf16[2,128,1152]{2,1,0:T(8,128)(2,1)S(1)}, bf16[2,128,1152]{2,1,0:T(8,128)(2,1)S(1)}, u32[]{:S(2)}, u32[]{:S(2)}) collective-permute-start(bf16[2,128,1152]{2,1,0:T(8,128)(2,1)S(1)} %pad_maximum_fusion), channel_id=1, source_target_pairs={{8,0},{10,2},{12,4},{14,6},{16,8},{18,10},{20,12},{22,14},{24,16},... | collective-permute-start | bytes 1769480 | tf_op jit(solution)/shard_map/ppermute | solution.py:11
  12.6 20.7 %collective-permute-start.6 = (bf16[2,128,1152]{2,1,0:T(8,128)(2,1)S(1)}, bf16[2,128,1152]{2,1,0:T(8,128)(2,1)S(1)}, u32[]{:S(2)}, u32[]{:S(2)}) collective-permute-start(bf16[2,128,1152]{2,1,0:T(8,128)(2,1)S(1)} %pad_maximum_fusion), channel_id=1, source_target_pairs={{6,0},{8,2},{10,4},{12,6},{14,8},{16,10},{18,12},{20,14},{22,16},{... | collective-permute-start | bytes 1769480 | tf_op jit(solution)/shard_map/ppermute | solution.py:11
  13.9 25.4 %collective-permute-start.5 = (bf16[2,128,1152]{2,1,0:T(8,128)(2,1)S(1)}, bf16[2,128,1152]{2,1,0:T(8,128)(2,1)S(1)}, u32[]{:S(2)}, u32[]{:S(2)}) collective-permute-start(bf16[2,128,1152]{2,1,0:T(8,128)(2,1)S(1)} %pad_maximum_fusion), channel_id=1, source_target_pairs={{4,0},{6,2},{8,4},{10,6},{12,8},{14,10},{16,12},{18,14},{20,16},{2... | collective-permute-start | bytes 1769480 | tf_op jit(solution)/shard_map/ppermute | solution.py:11
  15.2 48.4 %collective-permute-start.4 = (bf16[2,128,1152]{2,1,0:T(8,128)(2,1)S(1)}, bf16[2,128,1152]{2,1,0:T(8,128)(2,1)S(1)}, u32[]{:S(2)}, u32[]{:S(2)}) collective-permute-start(bf16[2,128,1152]{2,1,0:T(8,128)(2,1)S(1)} %pad_maximum_fusion), channel_id=1, source_target_pairs={{2,0},{4,2},{6,4},{8,6},{10,8},{12,10},{14,12},{16,14},{18,16},{20... | collective-permute-start | bytes 1769480 | tf_op jit(solution)/shard_map/ppermute | solution.py:11
  16.5 47.1 %collective-permute-start.3 = (bf16[2,128,1152]{2,1,0:T(8,128)(2,1)S(1)}, bf16[2,128,1152]{2,1,0:T(8,128)(2,1)S(1)}, u32[]{:S(2)}, u32[]{:S(2)}) collective-permute-start(bf16[2,128,1152]{2,1,0:T(8,128)(2,1)S(1)} %pad_maximum_fusion), channel_id=1, source_target_pairs={{0,2},{2,4},{4,6},{6,8},{8,10},{10,12},{12,14},{14,16},{16,18},{18... | collective-permute-start | bytes 1769480 | tf_op jit(solution)/shard_map/ppermute | solution.py:11
  23.1 52.6 %copy-start.2 = (bf16[16,128,1152]{2,1,0:T(8,128)(2,1)}, bf16[16,128,1152]{2,1,0:T(8,128)(2,1)S(1)}, u32[]{:S(2)}) copy-start(bf16[16,128,1152]{2,1,0:T(8,128)(2,1)S(1)} %broadcast_select_fusion) | copy-start | bytes 14155780
  30.4 37.5 %collective-permute-start.2 = (bf16[2,128,1152]{2,1,0:T(8,128)(2,1)S(1)}, bf16[2,128,1152]{2,1,0:T(8,128)(2,1)S(1)}, u32[]{:S(2)}, u32[]{:S(2)}) collective-permute-start(bf16[2,128,1152]{2,1,0:T(8,128)(2,1)S(1)} %pad_maximum_fusion), channel_id=1, source_target_pairs={{0,4},{2,6},{4,8},{6,10},{8,12},{10,14},{12,16},{14,18},{16,20},{1... | collective-permute-start | bytes 1769480 | tf_op jit(solution)/shard_map/ppermute | solution.py:11
  33.3 41.0 %collective-permute-start.1 = (bf16[2,128,1152]{2,1,0:T(8,128)(2,1)S(1)}, bf16[2,128,1152]{2,1,0:T(8,128)(2,1)S(1)}, u32[]{:S(2)}, u32[]{:S(2)}) collective-permute-start(bf16[2,128,1152]{2,1,0:T(8,128)(2,1)S(1)} %pad_maximum_fusion), channel_id=1, source_target_pairs={{0,6},{2,8},{4,10},{6,12},{8,14},{10,16},{12,18},{14,20},{16,22},{... | collective-permute-start | bytes 1769480 | tf_op jit(solution)/shard_map/ppermute | solution.py:11
  39.3 35.0 %collective-permute-start = (bf16[2,128,1152]{2,1,0:T(8,128)(2,1)S(1)}, bf16[2,128,1152]{2,1,0:T(8,128)(2,1)S(1)}, u32[]{:S(2)}, u32[]{:S(2)}) collective-permute-start(bf16[2,128,1152]{2,1,0:T(8,128)(2,1)S(1)} %pad_maximum_fusion), channel_id=1, source_target_pairs={{0,8},{2,10},{4,12},{6,14},{8,16},{10,18},{12,20},{14,22},{16,24},... | collective-permute-start | bytes 1769480 | tf_op jit(solution)/shard_map/ppermute | solution.py:11
  74.4 1.0 copy-start.3
  74.4 1.0 copy-start.4
  84.4 276.4 %reduce-scatter.2.cloned.1.call-start = ((), (), s32[]{:S(2)}) async-start(), calls=%async_computation.2 | async-start | bytes 884736 | tf_op jit(solution)/shard_map/reduce_scatter | solution.py:84
  242.8 17.1 %collective-permute-start.15 = (f32[128,1152]{1,0:T(8,128)S(1)}, f32[128,1152]{1,0:T(8,128)S(1)}, u32[]{:S(2)}, u32[]{:S(2)}) collective-permute-start(f32[128,1152]{1,0:T(8,128)S(1)} %concatenate.94), channel_id=1, source_target_pairs={{0,8},{2,10},{4,12},{6,14},{8,16},{10,18},{12,20},{14,22},{16,24},... | collective-permute-start | bytes 1769480 | tf_op jit(solution)/shard_map/ppermute | solution.py:11
  246.2 18.1 %collective-permute-start.8 = (f32[128,1152]{1,0:T(8,128)S(1)}, f32[128,1152]{1,0:T(8,128)S(1)}, u32[]{:S(2)}, u32[]{:S(2)}) collective-permute-start(f32[128,1152]{1,0:T(8,128)S(1)} %concatenate.87), channel_id=1, source_target_pairs={{8,0},{10,2},{12,4},{14,6},{16,8},{18,10},{20,12},{22,14},{24,16},... | collective-permute-start | bytes 1769480 | tf_op jit(solution)/shard_map/ppermute | solution.py:11
  247.6 18.1 %collective-permute-start.14 = (f32[128,1152]{1,0:T(8,128)S(1)}, f32[128,1152]{1,0:T(8,128)S(1)}, u32[]{:S(2)}, u32[]{:S(2)}) collective-permute-start(f32[128,1152]{1,0:T(8,128)S(1)} %concatenate.93), channel_id=1, source_target_pairs={{0,6},{2,8},{4,10},{6,12},{8,14},{10,16},{12,18},{14,20},{16,22},{... | collective-permute-start | bytes 1769480 | tf_op jit(solution)/shard_map/ppermute | solution.py:11
  250.0 17.0 %collective-permute-start.9 = (f32[128,1152]{1,0:T(8,128)S(1)}, f32[128,1152]{1,0:T(8,128)S(1)}, u32[]{:S(2)}, u32[]{:S(2)}) collective-permute-start(f32[128,1152]{1,0:T(8,128)S(1)} %concatenate.88), channel_id=1, source_target_pairs={{6,0},{8,2},{10,4},{12,6},{14,8},{16,10},{18,12},{20,14},{22,16},{... | collective-permute-start | bytes 1769480 | tf_op jit(solution)/shard_map/ppermute | solution.py:11
  251.5 43.2 %collective-permute-start.13 = (f32[128,1152]{1,0:T(8,128)S(1)}, f32[128,1152]{1,0:T(8,128)S(1)}, u32[]{:S(2)}, u32[]{:S(2)}) collective-permute-start(f32[128,1152]{1,0:T(8,128)S(1)} %concatenate.92), channel_id=1, source_target_pairs={{0,4},{2,6},{4,8},{6,10},{8,12},{10,14},{12,16},{14,18},{16,20},{1... | collective-permute-start | bytes 1769480 | tf_op jit(solution)/shard_map/ppermute | solution.py:11
  259.9 34.8 %collective-permute-start.10 = (f32[128,1152]{1,0:T(8,128)S(1)}, f32[128,1152]{1,0:T(8,128)S(1)}, u32[]{:S(2)}, u32[]{:S(2)}) collective-permute-start(f32[128,1152]{1,0:T(8,128)S(1)} %concatenate.89), channel_id=1, source_target_pairs={{4,0},{6,2},{8,4},{10,6},{12,8},{14,10},{16,12},{18,14},{20,16},{2... | collective-permute-start | bytes 1769480 | tf_op jit(solution)/shard_map/ppermute | solution.py:11
  264.3 30.4 %collective-permute-start.12 = (f32[128,1152]{1,0:T(8,128)S(1)}, f32[128,1152]{1,0:T(8,128)S(1)}, u32[]{:S(2)}, u32[]{:S(2)}) collective-permute-start(f32[128,1152]{1,0:T(8,128)S(1)} %concatenate.91), channel_id=1, source_target_pairs={{0,2},{2,4},{4,6},{6,8},{8,10},{10,12},{12,14},{14,16},{16,18},{18... | collective-permute-start | bytes 1769480 | tf_op jit(solution)/shard_map/ppermute | solution.py:11
  265.6 29.0 %collective-permute-start.11 = (f32[128,1152]{1,0:T(8,128)S(1)}, f32[128,1152]{1,0:T(8,128)S(1)}, u32[]{:S(2)}, u32[]{:S(2)}) collective-permute-start(f32[128,1152]{1,0:T(8,128)S(1)} %concatenate.90), channel_id=1, source_target_pairs={{2,0},{4,2},{6,4},{8,6},{10,8},{12,10},{14,12},{16,14},{18,16},{20... | collective-permute-start | bytes 1769480 | tf_op jit(solution)/shard_map/ppermute | solution.py:11
  311.5 51.1 %copy-start.1 = (bf16[16,32]{1,0:T(8,128)(2,1)S(1)}, bf16[16,32]{1,0:T(8,128)(2,1)}, u32[]{:S(2)}) copy-start(bf16[16,32]{1,0:T(8,128)(2,1)} %param.9) | copy-start | bytes 3076
Sparse Core Ops, SparseCore 0:
  84.5 122.4 all-gather.1
  295.9 25.7 reduce-scatter.1
where the time goes:
time: 370 us; the launch traced here: 369 us
  waiting for transfers between devices  174 us (47%)
  starting transfers between devices  58 us (16%)
  matrix products  44.4 us (12%)
  blocking collectives  40.9 us (11%)
  local copies, waits for them, and re-layouts  25.8 us (7%)
  between operations  14.7 us (4%)
  other arithmetic  11.1 us (3%)
    all_gather x1, waiting for transfers between devices, body(): piece = lax.all_gather(partner, 'aux', axis=0, tiled=True)  122 us
    ppermute x16, starting transfers between devices, passed_along(): return lax.ppermute(block, axis, route)  57.8 us
    ppermute x16, waiting for transfers between devices, passed_along(): return lax.ppermute(block, axis, route)  52.1 us
    psum x1, blocking collectives, body(): lax.psum(polar_part, 'chain')  40.9 us
    unnamed x24, local copies, waits for them, and re-layouts  13.9 us
    dot_general x1, matrix products, body(): jnp.dot(screened, stack_occ, preferred_element_type=jnp.float32)  10.4 us
    dot_general x1, matrix products, body(): lax.dot_general(screened, response, (((0,), (0,)), ((), ())), preferred_e...  10.3 us
    dot_general x1, matrix products, body(): jnp.dot(screened, stack_vir, preferred_element_type=jnp.float32)  8.63 us
  transfers between devices with their start and end apart: 18, of which 7 were waited for; matrix products, arithmetic and copies ran while one was open for 8% of the time, Pallas kernels for 0%

commit v1 on v0

--- a/solution.py
+++ b/solution.py
@@ -59,7 +59,9 @@
     coupled = coupled.reshape(aux_here, block_size * band_cols)
     partner = jnp.dot(screened, stack_vir, preferred_element_type=jnp.float32).astype(jnp.bfloat16)
     partner = partner.reshape(aux_here, block_size, band_cols)
-    piece = lax.all_gather(partner, "aux", axis=0, tiled=True)
+    piece = jnp.concatenate(
+        lax.all_to_all(jnp.stack([partner] * lax.axis_size("aux")), "aux", 0, 0), axis=0
+    )
     piece_rows = piece.shape[0]
     columns = piece.reshape(piece_rows, block_size * band_cols)
     products = lax.dot_general(

time: 370 us -> 377 us (1.019)
  blocking collectives: 40.9 us -> 139 us
  waiting for transfers between devices: 174 us -> 84.5 us
  starting transfers between devices: 58 us -> 48.5 us
  other arithmetic: 11.1 us -> 19.5 us
    all_gather x1 -> x0, waiting for transfers between devices: 122 us -> none  [body(): piece = lax.all_gather(partner, 'aux', axis=0, tiled=True)]
    all_to_all x0 -> x1, blocking collectives: none -> 109 us  [body(): lax.all_to_all(jnp.stack([partner] * lax.axis_size('aux')), 'aux', 0, 0)]
    ppermute x16, waiting for transfers between devices: 52.1 us -> 84.5 us  [passed_along(): return lax.ppermute(block, axis, route)]
    psum x1, blocking collectives: 40.9 us -> 30 us  [body(): lax.psum(polar_part, 'chain')]
    ppermute x16, starting transfers between devices: 57.8 us -> 48.5 us  [passed_along(): return lax.ppermute(block, axis, route)]
    another operation x0 -> x1, other arithmetic: none -> 8.35 us  [body(): jnp.stack([partner] * lax.axis_size('aux'))]
  transfers between devices with their start and end apart: 18 -> 17, of which waited for: 7 -> 6; matrix products, arithmetic and copies ran while one was open for 8% -> 8% of each run, Pallas kernels for 0% -> 0%
where the time goes in v1:
time: 377 us; the launch traced here: 376 us
  blocking collectives  139 us (37%)
  waiting for transfers between devices  84.5 us (22%)
  starting transfers between devices  48.5 us (13%)
  matrix products  44.2 us (12%)
  local copies, waits for them, and re-layouts  25.1 us (7%)
  other arithmetic  19.5 us (5%)
  between operations  14.7 us (4%)
    all_to_all x1, blocking collectives, body(): lax.all_to_all(jnp.stack([partner] * lax.axis_size('aux')), 'aux', 0, 0)  109 us
    ppermute x16, waiting for transfers between devices, passed_along(): return lax.ppermute(block, axis, route)  84.5 us
    ppermute x16, starting transfers between devices, passed_along(): return lax.ppermute(block, axis, route)  48.5 us
    psum x1, blocking collectives, body(): lax.psum(polar_part, 'chain')  30 us
    unnamed x24, local copies, waits for them, and re-layouts  13.2 us
    dot_general x1, matrix products, body(): jnp.dot(screened, stack_occ, preferred_element_type=jnp.float32)  10.4 us
    dot_general x1, matrix products, body(): lax.dot_general(screened, response, (((0,), (0,)), ((), ())), preferred_e...  10.3 us
    dot_general x1, matrix products, body(): jnp.dot(screened, stack_vir, preferred_element_type=jnp.float32)  8.56 us
  transfers between devices with their start and end apart: 17, of which 6 were waited for; matrix products, arithmetic and copies ran while one was open for 8% of the time, Pallas kernels for 0%

profile of v1, /device:TPU:0, one launch (start us, length us, event | category | flops | bytes accessed | tf_op | source)
XLA Modules:
  0.0 375.5 jit_solution(5415388500980510361)
XLA Ops:
  7.2 1.3 fusion.12
  11.3 5.0 %collective-permute-start = (bf16[2,128,1152]{2,1,0:T(8,128)(2,1)S(1)}, bf16[2,128,1152]{2,1,0:T(8,128)(2,1)S(1)}, u32[]{:S(2)}, u32[]{:S(2)}) collective-permute-start(bf16[2,128,1152]{2,1,0:T(8,128)(2,1)S(1)} %pad_maximum_fusion.1), channel_id=1, source_target_pairs={{0,8},{2,10},{4,12},{6,14},{8,16},{10,18},{12,20},{14,22},{16,24},... | collective-permute-start | bytes 1769480 | tf_op jit(solution)/shard_map/ppermute | solution.py:11
  16.3 2.6 collective-permute-start.1
  18.9 3.4 collective-permute-start.2
  22.4 2.6 collective-permute-start.3
  25.0 1.3 collective-permute-start.4
  27.1 2.8 broadcast_select_fusion
  31.3 1.3 collective-permute-start.6
  32.7 34.4 %collective-permute-done.2 = bf16[2,128,1152]{2,1,0:T(8,128)(2,1)S(1)} collective-permute-done((bf16[2,128,1152]{2,1,0:T(8,128)(2,1)S(1)}, bf16[2,128,1152]{2,1,0:T(8,128)(2,1)S(1)}, u32[]{:S(2)}, u32[]{:S(2)}) %collective-permute-start.2) | collective-permute-done | bytes 589856 | tf_op jit(solution)/shard_map/ppermute | solution.py:11
  69.1 9.8 %collective-permute-done.7 = bf16[2,128,1152]{2,1,0:T(8,128)(2,1)S(1)} collective-permute-done((bf16[2,128,1152]{2,1,0:T(8,128)(2,1)S(1)}, bf16[2,128,1152]{2,1,0:T(8,128)(2,1)S(1)}, u32[]{:S(2)}, u32[]{:S(2)}) %collective-permute-start.7) | collective-permute-done | bytes 589856 | tf_op jit(solution)/shard_map/ppermute | solution.py:11
  79.5 8.6 %convolution_convert_fusion.2 = bf16[2048,1152]{1,0:T(8,128)(2,1)} fusion(bf16[2048,1152]{1,0:T(8,128)(2,1)S(1)} %bitcast.59, bf16[1152,1152]{1,0:T(8,128)(2,1)S(1)} %pad_dynamic-update-slice_fusion.8), kind=kOutput, calls=%fused_computation.4 | convolution fusion | flops 5438177280 | bytes 12091392 | tf_op jit(solution)/shard_map/dot_general | solution.py:60
  88.0 8.4 %pad_maximum_fusion = bf16[2,16,128,1152]{3,2,1,0:T(8,128)(2,1)} fusion(bf16[1,16,128,1152]{3,2,1,0:T(8,128)(2,1)} %bitcast.58), kind=kLoop, calls=%fused_computation.2 | loop fusion | flops 4718592 | bytes 14155776 | tf_op jit(solution)/shard_map/stack | solution.py:63
  96.4 109.1 %all_to_all.5 = bf16[2,16,128,1152]{3,2,1,0:T(8,128)(2,1)} all-to-all(bf16[2,16,128,1152]{3,2,1,0:T(8,128)(2,1)} %pad_maximum_fusion), channel_id=1, replica_groups=mesh['chain'=16,'aux'=2] {'aux'}, dimensions={0} | all-to-all | bytes 18874368 | tf_op jit(solution)/shard_map/all_to_all | solution.py:63
  205.5 12.8 %copy.8 = bf16[4,8,128,1152]{3,1,2,0:T(8,128)(2,1)} copy(bf16[4,8,128,1152]{3,2,1,0:T(8,128)(2,1)} %bitcast.57) | data formatting | bytes 18874368
  218.2 7.2 %fusion = bf16[16,147456]{1,0:T(8,128)(2,1)} fusion(bf16[16,32]{1,0:T(8,128)(2,1)S(1)} %copy-done, bf16[32,147456]{1,0:T(8,128)(2,1)} %bitcast.55), kind=kOutput, calls=%fused_computation.1 | convolution fusion | flops 153354240 | bytes 14156800 | tf_op jit(solution)/shard_map/dot_general | solution.py:71
  225.4 5.2 %reshape.71 = bf16[2048,1152]{1,0:T(8,128)(2,1)} reshape(bf16[16,147456]{1,0:T(8,128)(2,1)} %fusion) | data formatting | bytes 9437184 | tf_op jit(solution)/shard_map/reshape | solution.py:76
  230.6 10.3 %fusion.17 = f32[1152,1152]{1,0:T(8,128)S(1)} fusion(bf16[2048,1152]{1,0:T(8,128)(2,1)} %bitcast.60, bf16[2048,1152]{1,0:T(8,128)(2,1)} %reshape.71), kind=kOutput, calls=%fused_computation.68 | convolution fusion | flops 5435817984 | bytes 14745600 | tf_op jit(solution)/shard_map/dot_general | solution.py:77
  241.2 1.3 collective-permute-start.11
  242.5 3.1 collective-permute-start.12
  245.7 1.3 collective-permute-start.10
  247.0 5.1 %collective-permute-start.13 = (f32[128,1152]{1,0:T(8,128)S(1)}, f32[128,1152]{1,0:T(8,128)S(1)}, u32[]{:S(2)}, u32[]{:S(2)}) collective-permute-start(f32[128,1152]{1,0:T(8,128)S(1)} %concatenate.92), channel_id=1, source_target_pairs={{0,4},{2,6},{4,8},{6,10},{8,12},{10,14},{12,16},{14,18},{16,20},{1... | collective-permute-start | bytes 1769480 | tf_op jit(solution)/shard_map/ppermute | solution.py:11
  252.3 11.6 %collective-permute-start.14 = (f32[128,1152]{1,0:T(8,128)S(1)}, f32[128,1152]{1,0:T(8,128)S(1)}, u32[]{:S(2)}, u32[]{:S(2)}) collective-permute-start(f32[128,1152]{1,0:T(8,128)S(1)} %concatenate.93), channel_id=1, source_target_pairs={{0,6},{2,8},{4,10},{6,12},{8,14},{10,16},{12,18},{14,20},{16,22},{... | collective-permute-start | bytes 1769480 | tf_op jit(solution)/shard_map/ppermute | solution.py:11
  264.1 1.3 collective-permute-start.9
  265.4 4.7 %collective-permute-start.15 = (f32[128,1152]{1,0:T(8,128)S(1)}, f32[128,1152]{1,0:T(8,128)S(1)}, u32[]{:S(2)}, u32[]{:S(2)}) collective-permute-start(f32[128,1152]{1,0:T(8,128)S(1)} %concatenate.94), channel_id=1, source_target_pairs={{0,8},{2,10},{4,12},{6,14},{8,16},{10,18},{12,20},{14,22},{16,24},... | collective-permute-start | bytes 1769480 | tf_op jit(solution)/shard_map/ppermute | solution.py:11
  271.6 6.4 %collective-permute-done.13 = f32[128,1152]{1,0:T(8,128)S(1)} collective-permute-done((f32[128,1152]{1,0:T(8,128)S(1)}, f32[128,1152]{1,0:T(8,128)S(1)}, u32[]{:S(2)}, u32[]{:S(2)}) %collective-permute-start.13) | collective-permute-done | bytes 589856 | tf_op jit(solution)/shard_map/ppermute | solution.py:11
  278.0 12.5 %collective-permute-done.14 = f32[128,1152]{1,0:T(8,128)S(1)} collective-permute-done((f32[128,1152]{1,0:T(8,128)S(1)}, f32[128,1152]{1,0:T(8,128)S(1)}, u32[]{:S(2)}, u32[]{:S(2)}) %collective-permute-start.14) | collective-permute-done | bytes 589856 | tf_op jit(solution)/shard_map/ppermute | solution.py:11
  290.5 21.3 %collective-permute-done.8 = f32[128,1152]{1,0:T(8,128)S(1)} collective-permute-done((f32[128,1152]{1,0:T(8,128)S(1)}, f32[128,1152]{1,0:T(8,128)S(1)}, u32[]{:S(2)}, u32[]{:S(2)}) %collective-permute-start.8) | collective-permute-done | bytes 589856 | tf_op jit(solution)/shard_map/ppermute | solution.py:11
  313.0 10.4 %convolution_convert_fusion.1 = bf16[2048,1152]{1,0:T(8,128)(2,1)} fusion(bf16[2048,1152]{1,0:T(8,128)(2,1)} %bitcast.61, bf16[1152,1152]{1,0:T(8,128)(2,1)S(1)} %pad_dynamic-update-slice_fusion), kind=kOutput, calls=%fused_computation.3 | convolution fusion | flops 5438177280 | bytes 12091392 | tf_op jit(solution)/shard_map/dot_general | solution.py:58
  323.4 5.2 %reshape.72 = bf16[16,147456]{1,0:T(8,128)(2,1)} reshape(bf16[2048,1152]{1,0:T(8,128)(2,1)} %convolution_convert_fusion.1) | data formatting | bytes 9437184 | tf_op jit(solution)/shard_map/reshape | solution.py:59
  328.6 7.7 %fusion.18 = f32[16,32]{1,0:T(8,128)S(1)} fusion(bf16[16,147456]{1,0:T(8,128)(2,1)} %reshape.72, bf16[32,147456]{1,0:T(8,128)(2,1)} %bitcast.56), kind=kOutput, calls=%fused_computation.69 | convolution fusion | flops 150994944 | bytes 14157824 | tf_op jit(solution)/shard_map/dot_general | solution.py:67
  336.4 30.0 %psum.7 = f32[16,32]{1,0:T(8,128)S(1)} all-reduce(f32[16,32]{1,0:T(8,128)S(1)} %fusion.18), channel_id=1, replica_groups=mesh['chain'=16,'aux'=2] {'chain'}, use_global_device_ids=true, to_apply=%region_3.4 | all-reduce | flops 512 | bytes 4096 | tf_op jit(solution)/shard_map/psum | solution.py:73
  367.0 1.7 select_multiply_fusion
  (89 shorter events, 11.1 us)
Async XLA Ops:
  7.2 211.1 %copy-start = (bf16[16,32]{1,0:T(8,128)(2,1)S(1)}, bf16[16,32]{1,0:T(8,128)(2,1)}, u32[]{:S(2)}) copy-start(bf16[16,32]{1,0:T(8,128)(2,1)} %param.9) | copy-start | bytes 3076
  7.2 359.8 %reduce-scatter.2.cloned.1.call-start = ((), (), s32[]{:S(2)}) async-start(), calls=%async_computation.2 | async-start | bytes 884736 | tf_op jit(solution)/shard_map/reduce_scatter | solution.py:86
  11.3 18.7 %collective-permute-start = (bf16[2,128,1152]{2,1,0:T(8,128)(2,1)S(1)}, bf16[2,128,1152]{2,1,0:T(8,128)(2,1)S(1)}, u32[]{:S(2)}, u32[]{:S(2)}) collective-permute-start(bf16[2,128,1152]{2,1,0:T(8,128)(2,1)S(1)} %pad_maximum_fusion.1), channel_id=1, source_target_pairs={{0,8},{2,10},{4,12},{6,14},{8,16},{10,18},{12,20},{14,22},{16,24},... | collective-permute-start | bytes 1769480 | tf_op jit(solution)/shard_map/ppermute | solution.py:11
  16.3 15.0 %collective-permute-start.1 = (bf16[2,128,1152]{2,1,0:T(8,128)(2,1)S(1)}, bf16[2,128,1152]{2,1,0:T(8,128)(2,1)S(1)}, u32[]{:S(2)}, u32[]{:S(2)}) collective-permute-start(bf16[2,128,1152]{2,1,0:T(8,128)(2,1)S(1)} %pad_maximum_fusion.1), channel_id=1, source_target_pairs={{0,6},{2,8},{4,10},{6,12},{8,14},{10,16},{12,18},{14,20},{16,22},{... | collective-permute-start | bytes 1769480 | tf_op jit(solution)/shard_map/ppermute | solution.py:11
  18.9 48.1 %collective-permute-start.2 = (bf16[2,128,1152]{2,1,0:T(8,128)(2,1)S(1)}, bf16[2,128,1152]{2,1,0:T(8,128)(2,1)S(1)}, u32[]{:S(2)}, u32[]{:S(2)}) collective-permute-start(bf16[2,128,1152]{2,1,0:T(8,128)(2,1)S(1)} %pad_maximum_fusion.1), channel_id=1, source_target_pairs={{0,4},{2,6},{4,8},{6,10},{8,12},{10,14},{12,16},{14,18},{16,20},{1... | collective-permute-start | bytes 1769480 | tf_op jit(solution)/shard_map/ppermute | solution.py:11
  22.4 46.0 %collective-permute-start.3 = (bf16[2,128,1152]{2,1,0:T(8,128)(2,1)S(1)}, bf16[2,128,1152]{2,1,0:T(8,128)(2,1)S(1)}, u32[]{:S(2)}, u32[]{:S(2)}) collective-permute-start(bf16[2,128,1152]{2,1,0:T(8,128)(2,1)S(1)} %pad_maximum_fusion.1), channel_id=1, source_target_pairs={{0,2},{2,4},{4,6},{6,8},{8,10},{10,12},{12,14},{14,16},{16,18},{18... | collective-permute-start | bytes 1769480 | tf_op jit(solution)/shard_map/ppermute | solution.py:11
  25.0 43.5 %collective-permute-start.4 = (bf16[2,128,1152]{2,1,0:T(8,128)(2,1)S(1)}, bf16[2,128,1152]{2,1,0:T(8,128)(2,1)S(1)}, u32[]{:S(2)}, u32[]{:S(2)}) collective-permute-start(bf16[2,128,1152]{2,1,0:T(8,128)(2,1)S(1)} %pad_maximum_fusion.1), channel_id=1, source_target_pairs={{2,0},{4,2},{6,4},{8,6},{10,8},{12,10},{14,12},{16,14},{18,16},{20... | collective-permute-start | bytes 1769480 | tf_op jit(solution)/shard_map/ppermute | solution.py:11
  29.9 49.6 %copy-start.2 = (bf16[16,128,1152]{2,1,0:T(8,128)(2,1)}, bf16[16,128,1152]{2,1,0:T(8,128)(2,1)S(1)}, u32[]{:S(2)}) copy-start(bf16[16,128,1152]{2,1,0:T(8,128)(2,1)S(1)} %broadcast_select_fusion) | copy-start | bytes 14155780
  30.0 38.6 %collective-permute-start.5 = (bf16[2,128,1152]{2,1,0:T(8,128)(2,1)S(1)}, bf16[2,128,1152]{2,1,0:T(8,128)(2,1)S(1)}, u32[]{:S(2)}, u32[]{:S(2)}) collective-permute-start(bf16[2,128,1152]{2,1,0:T(8,128)(2,1)S(1)} %pad_maximum_fusion.1), channel_id=1, source_target_pairs={{4,0},{6,2},{8,4},{10,6},{12,8},{14,10},{16,12},{18,14},{20,16},{2... | collective-permute-start | bytes 1769480 | tf_op jit(solution)/shard_map/ppermute | solution.py:11
  31.3 37.3 %collective-permute-start.6 = (bf16[2,128,1152]{2,1,0:T(8,128)(2,1)S(1)}, bf16[2,128,1152]{2,1,0:T(8,128)(2,1)S(1)}, u32[]{:S(2)}, u32[]{:S(2)}) collective-permute-start(bf16[2,128,1152]{2,1,0:T(8,128)(2,1)S(1)} %pad_maximum_fusion.1), channel_id=1, source_target_pairs={{6,0},{8,2},{10,4},{12,6},{14,8},{16,10},{18,12},{20,14},{22,16},{... | collective-permute-start | bytes 1769480 | tf_op jit(solution)/shard_map/ppermute | solution.py:11
  67.1 11.8 %collective-permute-start.7 = (bf16[2,128,1152]{2,1,0:T(8,128)(2,1)S(1)}, bf16[2,128,1152]{2,1,0:T(8,128)(2,1)S(1)}, u32[]{:S(2)}, u32[]{:S(2)}) collective-permute-start(bf16[2,128,1152]{2,1,0:T(8,128)(2,1)S(1)} %pad_maximum_fusion.1), channel_id=1, source_target_pairs={{8,0},{10,2},{12,4},{14,6},{16,8},{18,10},{20,12},{22,14},{24,16},... | collective-permute-start | bytes 1769480 | tf_op jit(solution)/shard_map/ppermute | solution.py:11
  69.0 10.1 %copy-start.3 = (bf16[128,1152]{1,0:T(8,128)(2,1)S(1)}, bf16[128,1152]{1,0:T(8,128)(2,1)}, u32[]{:S(2)}) copy-start(bf16[128,1152]{1,0:T(8,128)(2,1)} %param.6) | copy-start | bytes 884740
  69.0 10.1 %copy-start.4 = (bf16[128,1152]{1,0:T(8,128)(2,1)S(1)}, bf16[128,1152]{1,0:T(8,128)(2,1)}, u32[]{:S(2)}) copy-start(bf16[128,1152]{1,0:T(8,128)(2,1)} %param.7) | copy-start | bytes 884740
  241.2 22.9 %collective-permute-start.11 = (f32[128,1152]{1,0:T(8,128)S(1)}, f32[128,1152]{1,0:T(8,128)S(1)}, u32[]{:S(2)}, u32[]{:S(2)}) collective-permute-start(f32[128,1152]{1,0:T(8,128)S(1)} %concatenate.90), channel_id=1, source_target_pairs={{2,0},{4,2},{6,4},{8,6},{10,8},{12,10},{14,12},{16,14},{18,16},{20... | collective-permute-start | bytes 1769480 | tf_op jit(solution)/shard_map/ppermute | solution.py:11
  242.5 22.9 %collective-permute-start.12 = (f32[128,1152]{1,0:T(8,128)S(1)}, f32[128,1152]{1,0:T(8,128)S(1)}, u32[]{:S(2)}, u32[]{:S(2)}) collective-permute-start(f32[128,1152]{1,0:T(8,128)S(1)} %concatenate.91), channel_id=1, source_target_pairs={{0,2},{2,4},{4,6},{6,8},{8,10},{10,12},{12,14},{14,16},{16,18},{18... | collective-permute-start | bytes 1769480 | tf_op jit(solution)/shard_map/ppermute | solution.py:11
  245.7 24.5 %collective-permute-start.10 = (f32[128,1152]{1,0:T(8,128)S(1)}, f32[128,1152]{1,0:T(8,128)S(1)}, u32[]{:S(2)}, u32[]{:S(2)}) collective-permute-start(f32[128,1152]{1,0:T(8,128)S(1)} %concatenate.89), channel_id=1, source_target_pairs={{4,0},{6,2},{8,4},{10,6},{12,8},{14,10},{16,12},{18,14},{20,16},{2... | collective-permute-start | bytes 1769480 | tf_op jit(solution)/shard_map/ppermute | solution.py:11
  247.0 31.0 %collective-permute-start.13 = (f32[128,1152]{1,0:T(8,128)S(1)}, f32[128,1152]{1,0:T(8,128)S(1)}, u32[]{:S(2)}, u32[]{:S(2)}) collective-permute-start(f32[128,1152]{1,0:T(8,128)S(1)} %concatenate.92), channel_id=1, source_target_pairs={{0,4},{2,6},{4,8},{6,10},{8,12},{10,14},{12,16},{14,18},{16,20},{1... | collective-permute-start | bytes 1769480 | tf_op jit(solution)/shard_map/ppermute | solution.py:11
  252.3 38.3 %collective-permute-start.14 = (f32[128,1152]{1,0:T(8,128)S(1)}, f32[128,1152]{1,0:T(8,128)S(1)}, u32[]{:S(2)}, u32[]{:S(2)}) collective-permute-start(f32[128,1152]{1,0:T(8,128)S(1)} %concatenate.93), channel_id=1, source_target_pairs={{0,6},{2,8},{4,10},{6,12},{8,14},{10,16},{12,18},{14,20},{16,22},{... | collective-permute-start | bytes 1769480 | tf_op jit(solution)/shard_map/ppermute | solution.py:11
  264.1 26.4 %collective-permute-start.9 = (f32[128,1152]{1,0:T(8,128)S(1)}, f32[128,1152]{1,0:T(8,128)S(1)}, u32[]{:S(2)}, u32[]{:S(2)}) collective-permute-start(f32[128,1152]{1,0:T(8,128)S(1)} %concatenate.88), channel_id=1, source_target_pairs={{6,0},{8,2},{10,4},{12,6},{14,8},{16,10},{18,12},{20,14},{22,16},{... | collective-permute-start | bytes 1769480 | tf_op jit(solution)/shard_map/ppermute | solution.py:11
  265.4 25.1 %collective-permute-start.15 = (f32[128,1152]{1,0:T(8,128)S(1)}, f32[128,1152]{1,0:T(8,128)S(1)}, u32[]{:S(2)}, u32[]{:S(2)}) collective-permute-start(f32[128,1152]{1,0:T(8,128)S(1)} %concatenate.94), channel_id=1, source_target_pairs={{0,8},{2,10},{4,12},{6,14},{8,16},{10,18},{12,20},{14,22},{16,24},... | collective-permute-start | bytes 1769480 | tf_op jit(solution)/shard_map/ppermute | solution.py:11
  270.1 41.7 %collective-permute-start.8 = (f32[128,1152]{1,0:T(8,128)S(1)}, f32[128,1152]{1,0:T(8,128)S(1)}, u32[]{:S(2)}, u32[]{:S(2)}) collective-permute-start(f32[128,1152]{1,0:T(8,128)S(1)} %concatenate.87), channel_id=1, source_target_pairs={{8,0},{10,2},{12,4},{14,6},{16,8},{18,10},{20,12},{22,14},{24,16},... | collective-permute-start | bytes 1769480 | tf_op jit(solution)/shard_map/ppermute | solution.py:11
  328.6 40.0 %copy-start.1 = (bf16[16,32]{1,0:T(8,128)(2,1)S(1)}, bf16[16,32]{1,0:T(8,128)(2,1)}, u32[]{:S(2)}) copy-start(bf16[16,32]{1,0:T(8,128)(2,1)} %param.9) | copy-start | bytes 3076
Sparse Core Ops, SparseCore 0:
  313.1 17.8 reduce-scatter.1
